TPU v7x, 256 devices: a whole 4x4x8 slice. The times are simulated.
256 devices in a mesh: tm: 32 (over x, z), tensor: 8 (over y, core).
Axes of the slice: x: 4, y: 4, z: 8, core: 2. Of those that a mesh axis runs over, the one named last changes fastest.
Arguments:
- latents: float32 [32, 640, 64], P('tm', 'tensor'), may hold values from -6 to 6
- residual: bfloat16 [32, 640, 5120], P('tm'), may hold values from -6 to 6
- timesteps: int32 [32], P('tm'), may hold values from 0 to 999
- step_sizes: float32 [32], P('tm'), may hold values from 0.015 to 0.06
- embed_weight: bfloat16 [64, 5120], replicated
- mod_weight: bfloat16 [3, 256, 5120], P(None, None, 'tensor'), may hold values from -0.75 to 0.75
- up_weight: bfloat16 [5120, 7168], P('tm', 'tensor'), may hold values from -0.078125 to 0.078125
- down_weight: bfloat16 [7168, 5120], P('tensor', 'tm'), may hold values from -0.0625 to 0.0625
- head_weight: bfloat16 [5120, 64], replicated, may hold values from -0.078125 to 0.078125
Outputs:
- drift: float32 [32, 640, 64], P('tm', 'tensor')
- new_latents: float32 [32, 640, 64], P('tm', 'tensor')
All inputs are finite; a program needn't handle non-finite values.
Results may differ from a plain program's by a relative error of at most 0.0085.
Values may be sent and summed in bfloat16 or wider, within the bound.
No kernel may reach another device: no remote copies, remote signals or barrier semaphores. Data moves between devices by JAX's collectives and lax.ppermute only.
A program may use at most 128 MiB of HBM per device.

v0:
```python
import math
import jax
import jax.numpy as jnp
from jax import lax
from jax.sharding import PartitionSpec as P


def prefix(part, axis, combine, identity):
    place = lax.axis_index(axis)
    gathered = lax.all_gather(part, axis)
    state = jnp.zeros_like(part) + jnp.asarray(identity, part.dtype)

    def one(hop, state):
        return combine(state, lax.dynamic_index_in_dim(gathered, hop, 0, False))

    return lax.fori_loop(0, place, one, state)


def normalize(values):
    centre = values - jnp.mean(values, axis=-1, keepdims=True)
    spread = jnp.mean(centre * centre, axis=-1, keepdims=True)
    return centre * lax.rsqrt(spread + 1e-06)


def time_features(stamps, width):
    half = width // 2
    freqs = jnp.exp(-math.log(10000.0) * jnp.arange(half, dtype=jnp.float32) / half)
    angles = stamps.astype(jnp.float32)[:, None] * freqs[None, :]
    return jnp.concatenate([jnp.cos(angles), jnp.sin(angles)], axis=-1)


def add_terms(earlier, later):
    return earlier + later


def local(
    latents,
    residual,
    timesteps,
    step_sizes,
    embed_weight,
    mod_weight,
    up_weight,
    down_weight,
    head_weight,
):
    feature = jax.nn.silu(time_features(timesteps, mod_weight.shape[1])).astype(jnp.bfloat16)[0]
    piece_mod = jnp.einsum("f,kfd->kd", feature, mod_weight, preferred_element_type=jnp.float32)
    modulation = lax.all_gather(piece_mod, "tensor", axis=1, tiled=True)
    latent = latents[0]
    stream = residual[0]
    latent_bf = latent.astype(jnp.bfloat16)
    own_rows = latent.shape[0]
    row_start = lax.axis_index("tensor") * own_rows
    own_stream = lax.dynamic_slice_in_dim(stream, row_start, own_rows, 0)
    hidden = own_stream.astype(jnp.float32) + jnp.dot(
        latent_bf, embed_weight, preferred_element_type=jnp.float32
    )
    local_normed = (normalize(hidden) * (1.0 + modulation[1]) + modulation[0]).astype(jnp.bfloat16)
    normed = lax.all_gather(local_normed, "tensor", axis=0, tiled=True)
    preact = jnp.dot(
        normed,
        lax.all_gather(up_weight, "tm", axis=0, tiled=True),
        preferred_element_type=jnp.float32,
    )
    activated = jax.nn.gelu(preact, approximate=True).astype(jnp.bfloat16)
    partial_sums = jnp.dot(
        activated,
        lax.all_gather(down_weight, "tm", axis=1, tiled=True),
        preferred_element_type=jnp.float32,
    )
    mixed = lax.psum_scatter(
        partial_sums.astype(jnp.bfloat16), "tensor", scatter_dimension=0, tiled=True
    ).astype(jnp.float32)
    updated = hidden + modulation[2] * mixed
    drift = jnp.dot(
        normalize(updated).astype(jnp.bfloat16), head_weight, preferred_element_type=jnp.float32
    )
    position = lax.axis_index("tm")
    first = (position == 0).astype(jnp.float32)
    term = first * latent - step_sizes[0] * drift
    earlier = prefix(term, "tm", add_terms, jnp.zeros_like(term))
    new_latent = earlier + term
    return (drift[None], new_latent[None])


def solution(mesh):
    in_specs = (
        P("tm", "tensor", None),
        P("tm", None, None),
        P("tm"),
        P("tm"),
        P(),
        P(None, None, "tensor"),
        P("tm", "tensor"),
        P("tensor", "tm"),
        P(),
    )
    out_specs = (P("tm", "tensor", None), P("tm", "tensor", None))
    return jax.shard_map(local, mesh=mesh, in_specs=in_specs, out_specs=out_specs, check_vma=False)
```

profile of v0, /device:TPU:6, one launch (start us, length us, event | category | flops | bytes accessed | tf_op | source)
XLA Modules:
  0.0 398.8 jit_solution(11767064728763271483)
XLA Ops:
  7.2 1.9 fusion.28
  9.2 0.3 multiply_reduce_fusion.1
  10.3 0.2 fusion.29
  10.5 13.3 %all_gather.18 = f32[3,5120]{1,0:T(4,128)S(1)} all-gather(f32[3,640]{1,0:T(4,128)S(1)} %bitcast.46), channel_id=1, replica_groups=mesh['tm'=32,'tensor'=8] {'tensor'}, dimensions={1}, use_global_device_ids=true | all-gather | bytes 69120 | tf_op jit(solution)/shard_map/all_gather | solution.py:49
  23.9 1.3 add_convert_fusion
  25.2 0.7 all-gather.8.cloned.1.call-update
  26.0 0.7 all-gather.10.cloned.1.call-update
  26.7 45.4 %all-gather.6.cloned.1.call-done = bf16[640,5120]{1,0:T(8,128)(2,1)} async-done(((bf16[80,5120]{1,0:T(8,128)(2,1)}), bf16[640,5120]{1,0:T(8,128)(2,1)}) %all-gather.6.cloned.1.call-update) | async-done | bytes 6553616 | tf_op jit(solution)/shard_map/all_gather | solution.py:60
  72.2 103.0 %all-gather.8.cloned.1.call-done = bf16[5120,896]{1,0:T(8,128)(2,1)} async-done(((bf16[160,896]{1,0:T(8,128)(2,1)}), bf16[5120,896]{1,0:T(8,128)(2,1)}) %all-gather.8.cloned.1.call-update) | async-done | bytes 9175056 | tf_op jit(solution)/shard_map/all_gather | solution.py:63
  175.2 12.7 %fusion.30 = f32[640,896]{1,0:T(8,128)} fusion(bf16[640,5120]{1,0:T(8,128)(2,1)} %all-gather.6.cloned.1.call-done, bf16[5120,896]{1,0:T(8,128)(2,1)} %all-gather.8.cloned.1.call-done), kind=kOutput, calls=%fused_computation.50 | convolution fusion | flops 5872025600 | bytes 18022400 | tf_op jit(solution)/shard_map/dot_general | solution.py:61
  187.9 89.2 %all-gather.10.cloned.1.call-done = bf16[896,5120]{0,1:T(8,128)(2,1)} async-done(((bf16[896,160]{0,1:T(8,128)(2,1)}), bf16[896,5120]{0,1:T(8,128)(2,1)}) %all-gather.10.cloned.1.call-update) | async-done | bytes 9175056 | tf_op jit(solution)/shard_map/all_gather | solution.py:69
  277.1 12.2 %convolution_convert_fusion = bf16[640,5120]{1,0:T(8,128)(2,1)} fusion(bf16[896,5120]{0,1:T(8,128)(2,1)} %all-gather.10.cloned.1.call-done, f32[640,896]{1,0:T(8,128)} %fusion.30), kind=kOutput, calls=%fused_computation.2 | convolution fusion | flops 5880463360 | bytes 18022400 | tf_op jit(solution)/shard_map/dot_general | solution.py:67
  289.9 44.7 %reduce-scatter.2.cloned.1.call-done = bf16[80,5120]{1,0:T(8,128)(2,1)} async-done(((bf16[640,5120]{1,0:T(8,128)(2,1)}), bf16[80,5120]{1,0:T(8,128)(2,1)}) %reduce-scatter.2.cloned.1.call-update) | async-done | bytes 819216 | tf_op jit(solution)/shard_map/reduce_scatter | solution.py:72
  334.6 1.5 fusion.16
  336.2 0.5 multiply_reduce_fusion
  336.7 0.6 copy-done.2
  337.3 0.6 fusion.13
  337.9 50.2 %all-gather.1 = f32[32,80,64]{1,2,0:T(8,128)S(1)} all-gather(f32[1,80,64]{1,2,0:T(8,128)S(1)} %fusion.19), channel_id=2, replica_groups=mesh['tm'=32,'tensor'=8] {'tm'}, dimensions={0}, use_global_device_ids=true | all-gather | bytes 675840 | tf_op jit(solution)/shard_map/all_gather | solution.py:10
  388.1 3.4 while.10
  388.2 0.1 copy.20
  388.3 0.1 copy.20
  388.4 0.1 copy.20
  389.4 0.1 copy.20
  391.6 0.6 add_bitcast_fusion
  (95 shorter events, 2.5 us)
Async XLA Ops:
  7.2 3.1 copy-start
  7.2 65.0 %all-gather.6.cloned.1.call-start = ((), (), s32[]{:S(2)}) async-start(), calls=%async_computation.1 | async-start | bytes 7372800 | tf_op jit(solution)/shard_map/all_gather | solution.py:60
  25.2 150.0 %all-gather.8.cloned.1.call-start = ((), (), s32[]{:S(2)}) async-start(), calls=%async_computation.2 | async-start | bytes 9461760 | tf_op jit(solution)/shard_map/all_gather | solution.py:63
  26.0 251.1 %all-gather.10.cloned.1.call-start = ((), (), s32[]{:S(2)}) async-start(), calls=%async_computation.3 | async-start | bytes 9461760 | tf_op jit(solution)/shard_map/all_gather | solution.py:69
  26.7 307.9 %reduce-scatter.2.cloned.1.call-start = ((), (), s32[]{:S(2)}) async-start(), calls=%async_computation.4 | async-start | bytes 7372800 | tf_op jit(solution)/shard_map/reduce_scatter | solution.py:72
  334.6 1.6 copy-start.1
  336.2 1.1 copy-start.2
  336.7 1.2 copy-start.3
  337.9 54.4 %copy-start.4 = (f32[80,64]{0,1:T(8,128)}, f32[80,64]{0,1:T(8,128)S(1)}, u32[]{:S(2)}) copy-start(f32[80,64]{0,1:T(8,128)S(1)} %fusion.13) | copy-start | bytes 61444
Sparse Core Ops, SparseCore 0:
  25.3 46.7 all-gather.5
  74.7 100.4 all-gather.7
  177.8 99.2 all-gather.9
  289.4 45.1 reduce-scatter.1
where the time goes:
time: 399 us
  waiting for transfers between devices  284 us (71%)
  blocking collectives  63.5 us (16%)
  matrix products  27.6 us (7%)
  between operations  15.2 us (4%)
  other arithmetic  4.66 us (1%)
    all_gather x1, waiting for transfers between devices, local(): lax.all_gather(up_weight, 'tm', axis=0, tiled=True)  103 us
    all_gather x1, waiting for transfers between devices, local(): lax.all_gather(down_weight, 'tm', axis=1, tiled=True)  89.2 us
    all_gather x1, blocking collectives, prefix(): gathered = lax.all_gather(part, axis)  50.2 us
    all_gather x1, waiting for transfers between devices, local(): normed = lax.all_gather(local_normed, 'tensor', axis=0, tiled=True)  45.4 us
    reduce_scatter x1, waiting for transfers between devices, local(): lax.psum_scatter(partial_sums.astype(jnp.bfloat16), 'tensor', scatter_dim...  44.7 us
    all_gather x1, blocking collectives, local(): modulation = lax.all_gather(piece_mod, 'tensor', axis=1, tiled=True)  13.3 us
    dot_general x1, matrix products, local(): jnp.dot(normed, lax.all_gather(up_weight, 'tm', axis=0, tiled=True), pref...  12.7 us
    dot_general x1, matrix products, local(): jnp.dot(activated, lax.all_gather(down_weight, 'tm', axis=1, tiled=True),...  12.2 us
  transfers between devices with their start and end apart: 4, of which 4 were waited for; matrix products, arithmetic and copies ran while one was open for 3% of the time, Pallas kernels for 0%

commit v1 on v0

--- a/solution.py
+++ b/solution.py
@@ -3,6 +3,31 @@
 import jax.numpy as jnp
 from jax import lax
 from jax.sharding import PartitionSpec as P
+
+
+def draw_ways(block_in):
+    axis_tag = "tensor"
+    small = lax.axis_size(axis_tag)
+    p_next = lax.axis_index(axis_tag)
+    e_now, front, local_next = (small, p_next, block_in.shape[0])
+    after = jnp.zeros(
+        [p * e_now if to_i == 0 else p for to_i, p in enumerate(block_in.shape)], block_in.dtype
+    )
+    big = lax.dynamic_update_slice_in_dim(after, block_in, front * local_next, axis=0)
+    u_next = odd = block_in
+    for no in [*range(1, e_now // 2 + 1)]:
+        u_next = lax.ppermute(
+            u_next, axis_tag, [(to_i, (to_i + 1) % e_now) for to_i in range(e_now)]
+        )
+        big = lax.dynamic_update_slice_in_dim(
+            big, u_next, (front - no) % e_now * local_next, axis=0
+        )
+        if 2 * no < e_now:
+            odd = lax.ppermute(odd, axis_tag, [(to_i, (to_i - 1) % e_now) for to_i in range(e_now)])
+            big = lax.dynamic_update_slice_in_dim(
+                big, odd, (front + no) % e_now * local_next, axis=0
+            )
+    return big
 
 
 def prefix(part, axis, combine, identity):
@@ -57,7 +82,7 @@
         latent_bf, embed_weight, preferred_element_type=jnp.float32
     )
     local_normed = (normalize(hidden) * (1.0 + modulation[1]) + modulation[0]).astype(jnp.bfloat16)
-    normed = lax.all_gather(local_normed, "tensor", axis=0, tiled=True)
+    normed = draw_ways(local_normed)
     preact = jnp.dot(
         normed,
         lax.all_gather(up_weight, "tm", axis=0, tiled=True),

time: 399 us -> 337 us (0.84)
  waiting for transfers between devices: 284 us -> 202 us
  local copies, waits for them, and re-layouts: 2.8 us -> 13.5 us
  starting transfers between devices: 0.16 us -> 8.99 us
    all_gather x1, waiting for transfers between devices: 103 us -> 30.2 us  [local(): lax.all_gather(up_weight, 'tm', axis=0, tiled=True)]
    all_gather x1 -> x0, waiting for transfers between devices: 45.4 us -> none  [local(): normed = lax.all_gather(local_normed, 'tensor', axis=0, tiled=True)]
    ppermute x0 -> x7, waiting for transfers between devices: none -> 36.7 us  [the longest x4 36.7 us: draw_ways(): lax.ppermute(u_next, axis_tag, [(to_i, (to_i + 1) % e_now) for to_i in ra...]
    ppermute x0 -> x7, starting transfers between devices: none -> 8.87 us  [the longest x3 8.52 us: draw_ways(): lax.ppermute(odd, axis_tag, [(to_i, (to_i - 1) % e_now) for to_i in range...]
    dynamic_update_slice x0 -> x7, local copies, waits for them, and re-layouts: none -> 7.84 us  [the longest x4 4.97 us: draw_ways(): lax.dynamic_update_slice_in_dim(big, u_next, (front - no) % e_now * local...]
  transfers between devices with their start and end apart: 4 -> 10, of which waited for: 4 -> 7; matrix products, arithmetic and copies ran while one was open for 3% -> 8% of each run, Pallas kernels for 0% -> 0%
where the time goes in v1:
time: 337 us
  waiting for transfers between devices  202 us (60%)
  blocking collectives  63.5 us (19%)
  matrix products  27.5 us (8%)
  between operations  15.2 us (5%)
  local copies, waits for them, and re-layouts  13.5 us (4%)
  starting transfers between devices  8.99 us (3%)
  other arithmetic  4.92 us (1%)
    all_gather x1, waiting for transfers between devices, local(): lax.all_gather(down_weight, 'tm', axis=1, tiled=True)  89.2 us
    all_gather x1, blocking collectives, prefix(): gathered = lax.all_gather(part, axis)  50.2 us
    reduce_scatter x1, waiting for transfers between devices, local(): lax.psum_scatter(partial_sums.astype(jnp.bfloat16), 'tensor', scatter_dim...  44.7 us
    ppermute x4, waiting for transfers between devices, draw_ways(): lax.ppermute(u_next, axis_tag, [(to_i, (to_i + 1) % e_now) for to_i in ra...  36.7 us
    all_gather x1, waiting for transfers between devices, local(): lax.all_gather(up_weight, 'tm', axis=0, tiled=True)  30.2 us
    all_gather x1, blocking collectives, local(): modulation = lax.all_gather(piece_mod, 'tensor', axis=1, tiled=True)  13.3 us
    dot_general x1, matrix products, local(): jnp.dot(normed, lax.all_gather(up_weight, 'tm', axis=0, tiled=True), pref...  12.7 us
    dot_general x1, matrix products, local(): jnp.dot(activated, lax.all_gather(down_weight, 'tm', axis=1, tiled=True),...  12.2 us
  transfers between devices with their start and end apart: 10, of which 7 were waited for; matrix products, arithmetic and copies ran while one was open for 8% of the time, Pallas kernels for 0%

profile of v1, /device:TPU:6, one launch (start us, length us, event | category | flops | bytes accessed | tf_op | source)
XLA Modules:
  0.0 336.9 jit_solution(8423143687398635617)
XLA Ops:
  9.7 13.3 %all_gather.15 = f32[3,5120]{1,0:T(4,128)S(1)} all-gather(f32[3,640]{1,0:T(4,128)S(1)} %bitcast.46), channel_id=1, replica_groups=mesh['tm'=32,'tensor'=8] {'tensor'}, dimensions={1}, use_global_device_ids=true | all-gather | bytes 69120 | tf_op jit(solution)/shard_map/all_gather | solution.py:74
  23.0 1.9 fusion.28
  25.3 3.5 %broadcast_in_dim.8 = bf16[640,5120]{1,0:T(8,128)(2,1)} broadcast(bf16[]{:T(256)} %constant.89.clone.1), dimensions={} | broadcast | bytes 6553602 | tf_op jit(solution)/shard_map/broadcast_in_dim | solution.py:13
  28.8 1.5 constant_dynamic-update-slice_fusion.7
  30.6 2.6 collective-permute-start.1
  33.3 10.3 %collective-permute-done = bf16[80,5120]{1,0:T(8,128)(2,1)} collective-permute-done((bf16[80,5120]{1,0:T(8,128)(2,1)}, bf16[80,5120]{1,0:T(8,128)(2,1)}, u32[]{:S(2)}, u32[]{:S(2)}) %collective-permute-start) | collective-permute-done | bytes 819232 | tf_op jit(solution)/shard_map/ppermute | solution.py:19
  43.6 3.0 collective-permute-start.3
  46.6 2.1 constant_dynamic-update-slice_fusion.6
  49.6 7.2 %collective-permute-done.2 = bf16[80,5120]{1,0:T(8,128)(2,1)S(1)} collective-permute-done((bf16[80,5120]{1,0:T(8,128)(2,1)}, bf16[80,5120]{1,0:T(8,128)(2,1)S(1)}, u32[]{:S(2)}, u32[]{:S(2)}) %collective-permute-start.2) | collective-permute-done | bytes 819232 | tf_op jit(solution)/shard_map/ppermute | solution.py:19
  56.8 3.0 collective-permute-start.5
  59.7 1.0 constant_dynamic-update-slice_fusion.4
  60.7 1.0 constant_dynamic-update-slice_fusion.3
  61.7 8.1 %collective-permute-done.4 = bf16[80,5120]{1,0:T(8,128)(2,1)S(1)} collective-permute-done((bf16[80,5120]{1,0:T(8,128)(2,1)S(1)}, bf16[80,5120]{1,0:T(8,128)(2,1)S(1)}, u32[]{:S(2)}, u32[]{:S(2)}) %collective-permute-start.4) | collective-permute-done | bytes 819232 | tf_op jit(solution)/shard_map/ppermute | solution.py:19
  69.8 1.0 constant_dynamic-update-slice_fusion.2
  71.7 11.1 %collective-permute-done.6 = bf16[80,5120]{1,0:T(8,128)(2,1)S(1)} collective-permute-done((bf16[80,5120]{1,0:T(8,128)(2,1)S(1)}, bf16[80,5120]{1,0:T(8,128)(2,1)S(1)}, u32[]{:S(2)}, u32[]{:S(2)}) %collective-permute-start.6) | collective-permute-done | bytes 819232 | tf_op jit(solution)/shard_map/ppermute | solution.py:19
  82.7 1.0 constant_dynamic-update-slice_fusion
  83.7 30.2 %all-gather.5.cloned.1.call-done = bf16[5120,896]{1,0:T(8,128)(2,1)} async-done(((bf16[160,896]{1,0:T(8,128)(2,1)}), bf16[5120,896]{1,0:T(8,128)(2,1)}) %all-gather.5.cloned.1.call-update) | async-done | bytes 9175056 | tf_op jit(solution)/shard_map/all_gather | solution.py:88
  113.9 12.7 %fusion.30 = f32[640,896]{1,0:T(8,128)} fusion(bf16[640,5120]{1,0:T(8,128)(2,1)} %constant_dynamic-update-slice_fusion, bf16[5120,896]{1,0:T(8,128)(2,1)} %all-gather.5.cloned.1.call-done), kind=kOutput, calls=%fused_computation.58 | convolution fusion | flops 5872025600 | bytes 18022400 | tf_op jit(solution)/shard_map/dot_general | solution.py:86
  126.6 89.2 %all-gather.7.cloned.1.call-done = bf16[896,5120]{0,1:T(8,128)(2,1)} async-done(((bf16[896,160]{0,1:T(8,128)(2,1)}), bf16[896,5120]{0,1:T(8,128)(2,1)}) %all-gather.7.cloned.1.call-update) | async-done | bytes 9175056 | tf_op jit(solution)/shard_map/all_gather | solution.py:94
  215.8 12.2 %convolution_convert_fusion = bf16[640,5120]{1,0:T(8,128)(2,1)} fusion(bf16[896,5120]{0,1:T(8,128)(2,1)} %all-gather.7.cloned.1.call-done, f32[640,896]{1,0:T(8,128)} %fusion.30), kind=kOutput, calls=%fused_computation.2 | convolution fusion | flops 5880463360 | bytes 18022400 | tf_op jit(solution)/shard_map/dot_general | solution.py:92
  228.6 44.7 %reduce-scatter.2.cloned.1.call-done = bf16[80,5120]{1,0:T(8,128)(2,1)} async-done(((bf16[640,5120]{1,0:T(8,128)(2,1)}), bf16[80,5120]{1,0:T(8,128)(2,1)}) %reduce-scatter.2.cloned.1.call-update) | async-done | bytes 819216 | tf_op jit(solution)/shard_map/reduce_scatter | solution.py:97
  273.4 1.6 fusion.16
  276.0 50.2 %all-gather.1 = f32[32,80,64]{1,2,0:T(8,128)S(1)} all-gather(f32[1,80,64]{1,2,0:T(8,128)S(1)} %fusion.19), channel_id=2, replica_groups=mesh['tm'=32,'tensor'=8] {'tm'}, dimensions={0}, use_global_device_ids=true | all-gather | bytes 675840 | tf_op jit(solution)/shard_map/all_gather | solution.py:35
  326.3 3.4 %while.10 = (s32[]{:T(128)}, f32[80,64]{1,0:T(8,128)S(1)}, s32[]{:T(128)}, f32[32,80,64]{1,2,0:T(8,128)S(1)}, s32[]{:T(128)}, /*index=5*/s32[]{:T(128)}, s32[]{:T(128)}) while((s32[]{:T(128)}, f32[80,64]{1,0:T(8,128)S(1)}, s32[]{:T(128)}, f32[32,80,64]{1,2,0:T(8,128)S(1)}, s32[]{:T(128)}, /*index=5*/s32[]{:T(128)}, s32[]{:T(128)}) %tuple.29), condition=%wide.region_6.7_spmd, body=%wide.region_5.6_spmd.sunk | while | flops 5125 | bytes 143475 | solution.py:41
  (114 shorter events, 8.6 us)
Async XLA Ops:
  7.2 2.3 copy-start
  7.2 106.7 %all-gather.5.cloned.1.call-start = ((), (), s32[]{:S(2)}) async-start(), calls=%async_computation.1 | async-start | bytes 9461760 | tf_op jit(solution)/shard_map/all_gather | solution.py:88
  7.9 207.9 %all-gather.7.cloned.1.call-start = ((), (), s32[]{:S(2)}) async-start(), calls=%async_computation.2 | async-start | bytes 9461760 | tf_op jit(solution)/shard_map/all_gather | solution.py:94
  8.7 264.7 %reduce-scatter.2.cloned.1.call-start = ((), (), s32[]{:S(2)}) async-start(), calls=%async_computation.3 | async-start | bytes 7372800 | tf_op jit(solution)/shard_map/reduce_scatter | solution.py:97
  30.3 13.3 %collective-permute-start = (bf16[80,5120]{1,0:T(8,128)(2,1)}, bf16[80,5120]{1,0:T(8,128)(2,1)}, u32[]{:S(2)}, u32[]{:S(2)}) collective-permute-start(bf16[80,5120]{1,0:T(8,128)(2,1)} %get-tuple-element.43), channel_id=1, source_target_pairs={{0,1},{1,2},{2,3},{3,4},{4,5},{5,6},{6,7},{7,0},{8,9},{9,10},{10,1... | collective-permute-start | bytes 2457608 | tf_op jit(solution)/shard_map/ppermute | solution.py:19
  30.6 13.0 %collective-permute-start.1 = (bf16[80,5120]{1,0:T(8,128)(2,1)}, bf16[80,5120]{1,0:T(8,128)(2,1)S(1)}, u32[]{:S(2)}, u32[]{:S(2)}) collective-permute-start(bf16[80,5120]{1,0:T(8,128)(2,1)} %get-tuple-element.43), channel_id=1, source_target_pairs={{0,7},{1,0},{2,1},{3,2},{4,3},{5,4},{6,5},{7,6},{8,15},{9,8},{10,9... | collective-permute-start | bytes 2457608 | tf_op jit(solution)/shard_map/ppermute | solution.py:26
  43.6 13.2 %collective-permute-start.2 = (bf16[80,5120]{1,0:T(8,128)(2,1)}, bf16[80,5120]{1,0:T(8,128)(2,1)S(1)}, u32[]{:S(2)}, u32[]{:S(2)}) collective-permute-start(bf16[80,5120]{1,0:T(8,128)(2,1)} %collective-permute-done), channel_id=1, source_target_pairs={{0,1},{1,2},{2,3},{3,4},{4,5},{5,6},{6,7},{7,0},{8,9},{9,10},{10,1... | collective-permute-start | bytes 2457608 | tf_op jit(solution)/shard_map/ppermute | solution.py:19
  43.6 13.2 %collective-permute-start.3 = (bf16[80,5120]{1,0:T(8,128)(2,1)S(1)}, bf16[80,5120]{1,0:T(8,128)(2,1)S(1)}, u32[]{:S(2)}, u32[]{:S(2)}) collective-permute-start(bf16[80,5120]{1,0:T(8,128)(2,1)S(1)} %collective-permute-done.1), channel_id=1, source_target_pairs={{0,7},{1,0},{2,1},{3,2},{4,3},{5,4},{6,5},{7,6},{8,15},{9,8},{10,9... | collective-permute-start | bytes 2457608 | tf_op jit(solution)/shard_map/ppermute | solution.py:26
  56.8 13.0 %collective-permute-start.4 = (bf16[80,5120]{1,0:T(8,128)(2,1)S(1)}, bf16[80,5120]{1,0:T(8,128)(2,1)S(1)}, u32[]{:S(2)}, u32[]{:S(2)}) collective-permute-start(bf16[80,5120]{1,0:T(8,128)(2,1)S(1)} %collective-permute-done.2), channel_id=1, source_target_pairs={{0,1},{1,2},{2,3},{3,4},{4,5},{5,6},{6,7},{7,0},{8,9},{9,10},{10,1... | collective-permute-start | bytes 2457608 | tf_op jit(solution)/shard_map/ppermute | solution.py:19
  56.8 13.9 %collective-permute-start.5 = (bf16[80,5120]{1,0:T(8,128)(2,1)S(1)}, bf16[80,5120]{1,0:T(8,128)(2,1)S(1)}, u32[]{:S(2)}, u32[]{:S(2)}) collective-permute-start(bf16[80,5120]{1,0:T(8,128)(2,1)S(1)} %collective-permute-done.3), channel_id=1, source_target_pairs={{0,7},{1,0},{2,1},{3,2},{4,3},{5,4},{6,5},{7,6},{8,15},{9,8},{10,9... | collective-permute-start | bytes 2457608 | tf_op jit(solution)/shard_map/ppermute | solution.py:26
  69.8 13.0 %collective-permute-start.6 = (bf16[80,5120]{1,0:T(8,128)(2,1)S(1)}, bf16[80,5120]{1,0:T(8,128)(2,1)S(1)}, u32[]{:S(2)}, u32[]{:S(2)}) collective-permute-start(bf16[80,5120]{1,0:T(8,128)(2,1)S(1)} %collective-permute-done.4), channel_id=1, source_target_pairs={{0,1},{1,2},{2,3},{3,4},{4,5},{5,6},{6,7},{7,0},{8,9},{9,10},{10,1... | collective-permute-start | bytes 2457608 | tf_op jit(solution)/shard_map/ppermute | solution.py:19
  273.4 1.6 copy-start.1
  273.4 2.1 copy-start.2
  275.0 1.0 copy-start.3
  276.0 54.4 %copy-start.4 = (f32[80,64]{0,1:T(8,128)}, f32[80,64]{0,1:T(8,128)S(1)}, u32[]{:S(2)}) copy-start(f32[80,64]{0,1:T(8,128)S(1)} %fusion.13) | copy-start | bytes 61444
Sparse Core Ops, SparseCore 0:
  10.6 103.2 all-gather.4
  116.5 99.2 all-gather.6
  228.1 45.2 reduce-scatter.1
